TPU v7x, 256 devices: a whole 4x4x8 slice. The times are simulated.
256 devices in a mesh: seq: 16 (over y, x), exp: 16 (over z, core), dp: 1.
Axes of the slice: x: 4, y: 4, z: 8, core: 2. Of those that a mesh axis runs over, the one named last changes fastest.
Arguments:
- tokens: bfloat16 [16, 64, 64, 1280], P(('dp', 'exp'), 'seq'), may hold values from -6 to 6
- expert_ids: int32 [16, 64, 64, 1], P(('dp', 'exp'), 'seq'), may hold values from 0 to 31; in each aligned block of 256 rows (0 to 255, 256 to 511, ..., all dimensions but the last counted through in order) at most 10 rows name the same one
- gate_values: float32 [16, 64, 64], P(('dp', 'exp'), 'seq'), may hold values from 0.25 to 1
- mixer_gain: float32 [1280], replicated, may hold values from 0.1 to 1.9
- expert_gain: float32 [1280], replicated, may hold values from 0.1 to 1.9
- conv_weight: float32 [3, 3, 1280], replicated, may hold values from -2 to 2
- conv_bias: float32 [1280], replicated, may hold values from -3 to 3
- w_in: bfloat16 [32, 1280, 5120], P('exp', None, 'seq'), may hold values from -0.15625 to 0.15625
- b_in: float32 [32, 5120], P('exp', 'seq'), may hold values from -3 to 3
- w_out: bfloat16 [32, 5120, 1280], P('exp', 'seq'), may hold values from -0.078125 to 0.078125
- b_out: float32 [32, 1280], P('exp'), may hold values from -3 to 3
Outputs:
- result: bfloat16 [16, 64, 64, 1280], P(('dp', 'exp'), 'seq')
Inputs may be any that keep to these rules, and one draw needn't show every extreme that they name: `expert_ids`: among the 256 patches of one image's block of 4 rows (rows k * 4 to k * 4 + 3), no expert is chosen more than 10 times, and in every draw some expert is chosen exactly 10 times in some block.
All inputs are finite; a program needn't handle non-finite values.
Results may differ from a plain program's by a relative error of at most 0.006.
Values may be sent and summed in bfloat16 or wider, within the bound.
No kernel may reach another device: no remote copies, remote signals or barrier semaphores. Data moves between devices by JAX's collectives and lax.ppermute only.
A program may use at most 128 MiB of HBM per device.

v0:
```python
import jax
import jax.numpy as jnp
from jax import lax
from jax.sharding import PartitionSpec as P


def with_halo(cells, sides, width):
    for axis, dim in sides:
        count = lax.axis_size(axis)
        ends = count - 1
        head = lax.slice_in_dim(cells, 0, width, axis=dim)
        tail = lax.slice_in_dim(cells, cells.shape[dim] - width, cells.shape[dim], axis=dim)
        cells = jnp.concatenate(
            [
                lax.ppermute(tail, axis, [(i, (i + 1) % count) for i in range(ends)]),
                cells,
                lax.ppermute(head, axis, [((i + 1) % count, i) for i in range(ends)]),
            ],
            axis=dim,
        )
    return cells


def normalize(values, scales):
    row_mean = jnp.mean(values, axis=-1, keepdims=True)
    centred = values - row_mean
    row_var = jnp.mean(centred * centred, axis=-1, keepdims=True)
    return centred * lax.rsqrt(row_var + 1e-06) * scales


def depthwise(padded, conv_weight, height, width):
    summed = padded[..., 0:height, 0:width, :] * conv_weight[0, 0]
    for row_off in range(3):
        for col_off in range(3):
            if row_off + col_off > 0:
                summed = (
                    summed
                    + padded[..., row_off : row_off + height, col_off : col_off + width, :]
                    * conv_weight[row_off, col_off]
                )
    return summed


def body(
    tokens,
    expert_ids,
    gate_values,
    mixer_gain,
    expert_gain,
    conv_weight,
    conv_bias,
    w_in,
    b_in,
    w_out,
    b_out,
):
    row_count = tokens.shape[1]
    col_count = tokens.shape[2]
    width_d = tokens.shape[3]
    values = tokens[0].astype(jnp.float32)
    normed = normalize(values, mixer_gain).astype(jnp.bfloat16)
    rim_source = tokens[0]
    extended = with_halo(rim_source, (("seq", 0),), 1)
    rim_rows = jnp.concatenate([extended[0:1], extended[row_count + 1 : row_count + 2]], axis=0)
    rim_rows = normalize(rim_rows.astype(jnp.float32), mixer_gain).astype(jnp.bfloat16)
    extended = jnp.concatenate([rim_rows[0:1], normed, rim_rows[1:2]], axis=0)
    padded = jnp.pad(extended.astype(jnp.float32), ((0, 0), (1, 1), (0, 0)))
    mixed = values + depthwise(padded, conv_weight, row_count, col_count) + conv_bias
    tok_rows = row_count * col_count
    expert_in = normalize(mixed, expert_gain).astype(jnp.bfloat16).reshape(tok_rows, width_d)
    per_device = w_in.shape[0]
    holders = lax.axis_size("exp")
    experts = per_device * holders
    slot_count = 5 * tok_rows // (4 * experts)
    route_ids = expert_ids.reshape(tok_rows)
    one_hot = (route_ids[:, None] == jnp.arange(experts, dtype=jnp.int32)[None, :]).astype(
        jnp.float32
    )
    positions = jnp.arange(tok_rows, dtype=jnp.int32)
    below_mask = (positions[:, None] > positions[None, :]).astype(jnp.float32)
    earlier = jnp.dot(below_mask, one_hot, precision=lax.Precision.HIGHEST)
    slot_rank = jnp.sum(earlier * one_hot, axis=1).astype(jnp.int32)
    column = (
        route_ids // per_device * slot_count + slot_rank
    ) * per_device + route_ids % per_device
    dispatch_mask = (
        column[:, None] == jnp.arange(experts * slot_count, dtype=jnp.int32)[None, :]
    ).astype(jnp.bfloat16)
    dispatched = jnp.einsum(
        "tk,td->kd", dispatch_mask, expert_in, preferred_element_type=jnp.float32
    ).astype(jnp.bfloat16)
    dispatched = dispatched.reshape(holders, slot_count, per_device, width_d)
    received = lax.all_to_all(dispatched, "exp", split_axis=0, concat_axis=0, tiled=True)
    gathered = lax.all_gather(received, "seq", axis=0, tiled=True)
    hidden = (
        jnp.einsum("kcjd,jdf->kcjf", gathered, w_in, preferred_element_type=jnp.float32)
        + b_in[None, None]
    )
    hidden = jax.nn.gelu(hidden, approximate=False).astype(jnp.bfloat16)
    summed = lax.psum_scatter(
        jnp.einsum("kcjf,jfd->kcjd", hidden, w_out, preferred_element_type=jnp.float32).astype(
            jnp.bfloat16
        ),
        "seq",
        scatter_dimension=0,
        tiled=True,
    ).astype(jnp.float32)
    back = (summed + b_out[None, None]).astype(jnp.bfloat16)
    returned = lax.all_to_all(back, "exp", split_axis=0, concat_axis=0, tiled=True).reshape(
        experts * slot_count, width_d
    )
    combined = jnp.dot(dispatch_mask, returned, preferred_element_type=jnp.float32)
    result = mixed.reshape(tok_rows, width_d) + gate_values.reshape(tok_rows)[:, None] * combined
    return result.astype(jnp.bfloat16).reshape(tokens.shape)


def solution(mesh):
    in_specs = (
        P(("dp", "exp"), "seq", None, None),
        P(("dp", "exp"), "seq", None, None),
        P(("dp", "exp"), "seq", None),
        P(),
        P(),
        P(),
        P(),
        P("exp", None, "seq"),
        P("exp", "seq"),
        P("exp", "seq", None),
        P("exp", None),
    )
    out_specs = P(("dp", "exp"), "seq", None, None)
    return jax.shard_map(body, mesh=mesh, in_specs=in_specs, out_specs=out_specs, check_vma=False)
```

profile of v0, /device:TPU:1, one launch (start us, length us, event | category | flops | bytes accessed | tf_op | source)
XLA Modules:
  0.0 334.6 jit_solution(12479019363799753572)
XLA Ops:
  6.5 1.1 slice_bitcast_fusion.1
  7.7 4.0 %collective-permute-start = (bf16[1,64,1280]{2,1,0:T(8,128)(2,1)S(1)}, bf16[1,64,1280]{2,1,0:T(8,128)(2,1)S(1)}, u32[]{:S(2)}, u32[]{:S(2)}) collective-permute-start(bf16[1,64,1280]{2,1,0:T(8,128)(2,1)S(1)} %get-tuple-element.16), channel_id=1, source_target_pairs={{0,16},{16,32},{32,48},{48,64},{64,80},{80,96},{96,112},{112,128},... | collective-permute-start | bytes 491528 | tf_op jit(solution)/shard_map/ppermute | solution.py:15
  11.7 1.3 collective-permute-start.1
  13.0 1.3 convert_reduce_fusion
  14.2 1.4 fusion.61
  15.6 0.5 broadcast.173
  16.2 1.3 reduce.22
  17.5 0.1 reshape.120
  17.6 0.2 fusion.79
  17.8 1.4 fusion.63
  19.2 1.0 slice_reduce_fusion.8
  20.2 0.1 convert_reduce_fusion.1
  20.4 0.2 fusion.82
  20.6 0.9 fusion.84
  21.6 0.2 maximum_convert_fusion
  21.8 1.7 fusion.119
  23.5 0.3 multiply_reduce_fusion
  23.8 0.2 multiply_convert_fusion
  24.0 1.4 convolution_convert_fusion
  25.4 2.9 reshape.122
  28.3 33.1 %all_to_all.10 = bf16[16,10,2,1280]{3,2,1,0:T(2,128)(2,1)S(1)} all-to-all(bf16[16,10,2,1280]{3,2,1,0:T(2,128)(2,1)} %reshape.122), channel_id=1, replica_groups=mesh['seq'=16,'exp'=16,'dp'=1] {'exp'}, dimensions={0} | all-to-all | bytes 1638400 | tf_op jit(solution)/shard_map/all_to_all | solution.py:93
  61.4 1.0 copy.19
  62.5 0.2 reduce-scatter.2.cloned.1.call-start
  62.7 95.3 %all-gather.2.cloned.1.call-done = bf16[256,10,2,1280]{3,0,1,2:T(8,128)(2,1)} async-done(((bf16[16,10,2,1280]{3,0,1,2:T(8,128)(2,1)}), bf16[256,10,2,1280]{3,0,1,2:T(8,128)(2,1)}) %all-gather.2.cloned.1.call-update) | async-done | bytes 13107216 | tf_op jit(solution)/shard_map/all_gather | solution.py:94
  158.0 29.0 %convert_bitcast_fusion = bf16[256,10,2,1280]{3,0,1,2:T(8,128)(2,1)} fusion(bf16[256,10,2,1280]{3,0,1,2:T(8,128)(2,1)} %all-gather.2.cloned.1.call-done, f32[2,320]{1,0:T(2,128)S(1)} %copy-done.6, bf16[2,320,1280]{2,1,0:T(8,128)(2,1)S(1)} %copy-done, bf16[2,1280,320]{1,2,0:T(8,128)(2,1)} %param.18), kind=kOutput, calls=%fused_computation | convolution fusion | flops 8503296000 | bytes 29493760 | tf_op jit(solution)/shard_map/kcjf,jfd->kcjd/dot_general | solution.py:101
  187.0 100.8 %reduce-scatter.2.cloned.1.call-done = bf16[16,10,2,1280]{3,0,1,2:T(8,128)(2,1)} async-done(((bf16[256,10,2,1280]{3,0,1,2:T(8,128)(2,1)}), bf16[16,10,2,1280]{3,0,1,2:T(8,128)(2,1)}) %reduce-scatter.2.cloned.1.call-update) | async-done | bytes 819216 | tf_op jit(solution)/shard_map/reduce_scatter | solution.py:100
  287.8 1.3 add_convert_fusion
  289.1 1.7 copy.20
  290.9 7.9 %all-to-all-start.1 = ((bf16[16,10,2,1280]{3,2,1,0:T(2,128)(2,1)}), bf16[16,10,2,1280]{3,2,1,0:T(2,128)(2,1)}, u32[]{:S(2)}, u32[]{:S(2)}) async-start(bf16[16,10,2,1280]{3,2,1,0:T(2,128)(2,1)} %copy.20), calls=%async_computation.2 | async-start | bytes 1638400 | tf_op jit(solution)/shard_map/all_to_all | solution.py:109
  298.9 23.3 %all-to-all-done.1 = bf16[16,10,2,1280]{3,2,1,0:T(2,128)(2,1)} async-done(((bf16[16,10,2,1280]{3,2,1,0:T(2,128)(2,1)}), bf16[16,10,2,1280]{3,2,1,0:T(2,128)(2,1)}, u32[]{:S(2)}, u32[]{:S(2)}) %all-to-all-start.1) | async-done | bytes 819232 | tf_op jit(solution)/shard_map/all_to_all | solution.py:109
  322.2 3.0 reshape.123
  325.2 2.5 fusion.53
  (28 shorter events, 0.2 us)
Async XLA Ops:
  6.5 151.5 %copy-start = (bf16[2,320,1280]{2,1,0:T(8,128)(2,1)S(1)}, bf16[2,320,1280]{2,1,0:T(8,128)(2,1)}, u32[]{:S(2)}) copy-start(bf16[2,320,1280]{2,1,0:T(8,128)(2,1)} %param.20) | copy-start | bytes 4915204
  6.5 15.2 %copy-start.4 = (f32[1280]{0:T(1024)S(1)}, f32[1280]{0:T(1024)}, u32[]{:S(2)}) copy-start(f32[1280]{0:T(1024)} %param.17) | copy-start | bytes 15364
  6.5 151.5 %all-gather.2.cloned.1.call-start = ((), (), s32[]{:S(2)}) async-start(), calls=%async_computation.3 | async-start | bytes 13926400 | tf_op jit(solution)/shard_map/all_gather | solution.py:94
  7.7 12.5 %collective-permute-start = (bf16[1,64,1280]{2,1,0:T(8,128)(2,1)S(1)}, bf16[1,64,1280]{2,1,0:T(8,128)(2,1)S(1)}, u32[]{:S(2)}, u32[]{:S(2)}) collective-permute-start(bf16[1,64,1280]{2,1,0:T(8,128)(2,1)S(1)} %get-tuple-element.16), channel_id=1, source_target_pairs={{0,16},{16,32},{32,48},{48,64},{64,80},{80,96},{96,112},{112,128},... | collective-permute-start | bytes 491528 | tf_op jit(solution)/shard_map/ppermute | solution.py:15
  11.7 8.6 %collective-permute-start.1 = (bf16[1,64,1280]{2,1,0:T(8,128)(2,1)S(1)}, bf16[1,64,1280]{2,1,0:T(8,128)(2,1)S(1)}, u32[]{:S(2)}, u32[]{:S(2)}) collective-permute-start(bf16[1,64,1280]{2,1,0:T(8,128)(2,1)S(1)} %get-tuple-element.17), channel_id=1, source_target_pairs={{16,0},{32,16},{48,32},{64,48},{80,64},{96,80},{112,96},{128,112},... | collective-permute-start | bytes 491528 | tf_op jit(solution)/shard_map/ppermute | solution.py:17
  17.6 4.2 %copy-start.1 = (bf16[1,4,64,1280]{3,2,1,0:T(8,128)(2,1)S(1)}, bf16[1,4,64,1280]{3,2,1,0:T(8,128)(2,1)}, u32[]{:S(2)}) copy-start(bf16[1,4,64,1280]{3,2,1,0:T(8,128)(2,1)} %param.11) | copy-start | bytes 1966084
  21.5 2.2 copy-start.3
  23.4 134.6 %copy-start.6 = (f32[2,320]{1,0:T(2,128)S(1)}, f32[2,320]{1,0:T(2,128)}, u32[]{:S(2)}) copy-start(f32[2,320]{1,0:T(2,128)} %param.19) | copy-start | bytes 7684
  62.5 225.4 %reduce-scatter.2.cloned.1.call-start = ((), (), s32[]{:S(2)}) async-start(), calls=%async_computation.4 | async-start | bytes 13926400 | tf_op jit(solution)/shard_map/reduce_scatter | solution.py:100
  187.0 100.9 %copy-start.2 = (f32[2,1280]{1,0:T(2,128)S(1)}, f32[2,1280]{1,0:T(2,128)}, u32[]{:S(2)}) copy-start(f32[2,1280]{1,0:T(2,128)} %param.21) | copy-start | bytes 30724
  187.0 111.8 %copy-start.5 = (f32[1,4,64]{2,1,0:T(4,128)S(1)}, f32[1,4,64]{2,1,0:T(4,128)}, u32[]{:S(2)}) copy-start(f32[1,4,64]{2,1,0:T(4,128)} %param.13) | copy-start | bytes 3076
  290.9 31.3 %all-to-all-start.1 = ((bf16[16,10,2,1280]{3,2,1,0:T(2,128)(2,1)}), bf16[16,10,2,1280]{3,2,1,0:T(2,128)(2,1)}, u32[]{:S(2)}, u32[]{:S(2)}) async-start(bf16[16,10,2,1280]{3,2,1,0:T(2,128)(2,1)} %copy.20), calls=%async_computation.2 | async-start | bytes 1638400 | tf_op jit(solution)/shard_map/all_to_all | solution.py:109
Sparse Core Ops, SparseCore 0:
  62.6 95.3 all-gather.1
  187.1 100.6 reduce-scatter.1
where the time goes:
time: 335 us
  waiting for transfers between devices  220 us (66%)
  matrix products  33.1 us (10%)
  blocking collectives  33.1 us (10%)
  between operations  13.6 us (4%)
  starting transfers between devices  13.4 us (4%)
  local copies, waits for them, and re-layouts  11.6 us (3%)
  other arithmetic  10.4 us (3%)
    reduce_scatter x1, waiting for transfers between devices, body(): lax.psum_scatter(jnp.einsum('kcjf,jfd->kcjd', hidden, w_out, preferred_el...  101 us
    all_gather x1, waiting for transfers between devices, body(): gathered = lax.all_gather(received, 'seq', axis=0, tiled=True)  95.3 us
    all_to_all x1, blocking collectives, body(): lax.all_to_all(dispatched, 'exp', split_axis=0, concat_axis=0, tiled=True)  33.1 us
    dot_general x1, matrix products, body(): jnp.einsum('kcjf,jfd->kcjd', hidden, w_out, preferred_element_type=jnp.fl...  29 us
    all_to_all x1, waiting for transfers between devices, body(): lax.all_to_all(back, 'exp', split_axis=0, concat_axis=0, tiled=True)  23.3 us
    all_to_all x1, starting transfers between devices, body(): lax.all_to_all(back, 'exp', split_axis=0, concat_axis=0, tiled=True)  7.91 us
  transfers between devices with their start and end apart: 5, of which 3 were waited for; matrix products, arithmetic and copies ran while one was open for 2% of the time, Pallas kernels for 0%

commit v1 on v0

--- a/solution.py
+++ b/solution.py
@@ -91,7 +91,10 @@
     ).astype(jnp.bfloat16)
     dispatched = dispatched.reshape(holders, slot_count, per_device, width_d)
     received = lax.all_to_all(dispatched, "exp", split_axis=0, concat_axis=0, tiled=True)
-    gathered = lax.all_gather(received, "seq", axis=0, tiled=True)
+    size = lax.axis_size("seq")
+    pieces = jnp.stack([received for _ in range(size)])
+    pieces = lax.all_to_all(pieces, "seq", split_axis=0, concat_axis=0)
+    gathered = jnp.concatenate(pieces, axis=0)
     hidden = (
         jnp.einsum("kcjd,jdf->kcjf", gathered, w_in, preferred_element_type=jnp.float32)
         + b_in[None, None]

time: 335 us -> 403 us (1.20)
  blocking collectives: 33.1 us -> 190 us
  waiting for transfers between devices: 220 us -> 118 us
  local copies, waits for them, and re-layouts: 11.6 us -> 24.1 us
    all_to_all x0 -> x1, blocking collectives: none -> 157 us  [body(): pieces = lax.all_to_all(pieces, 'seq', split_axis=0, concat_axis=0)]
    all_gather x1 -> x0, waiting for transfers between devices: 95.3 us -> none  [body(): gathered = lax.all_gather(received, 'seq', axis=0, tiled=True)]
    another operation x0 -> x1, local copies, waits for them, and re-layouts: none -> 7.28 us  [body(): pieces = jnp.stack([received for _ in range(size)])]
    reduce_scatter x1, waiting for transfers between devices: 101 us -> 94.8 us  [body(): lax.psum_scatter(jnp.einsum('kcjf,jfd->kcjd', hidden, w_out, preferred_el...]
    all_to_all x0 -> x1, local copies, waits for them, and re-layouts: none -> 5.23 us  [body(): pieces = lax.all_to_all(pieces, 'seq', split_axis=0, concat_axis=0)]
  transfers between devices with their start and end apart: 5 -> 4, of which waited for: 3 -> 2; matrix products, arithmetic and copies ran while one was open for 2% -> 2% of each run, Pallas kernels for 0% -> 0%
where the time goes in v1:
time: 403 us; the launch traced here: 402 us
  blocking collectives  190 us (47%)
  waiting for transfers between devices  118 us (29%)
  matrix products  33.1 us (8%)
  local copies, waits for them, and re-layouts  24.1 us (6%)
  between operations  13.5 us (3%)
  starting transfers between devices  13.1 us (3%)
  other arithmetic  10.4 us (3%)
    all_to_all x1, blocking collectives, body(): pieces = lax.all_to_all(pieces, 'seq', split_axis=0, concat_axis=0)  157 us
    reduce_scatter x1, waiting for transfers between devices, body(): lax.psum_scatter(jnp.einsum('kcjf,jfd->kcjd', hidden, w_out, preferred_el...  94.8 us
    all_to_all x1, blocking collectives, body(): lax.all_to_all(dispatched, 'exp', split_axis=0, concat_axis=0, tiled=True)  33.1 us
    dot_general x1, matrix products, body(): jnp.einsum('kcjf,jfd->kcjd', hidden, w_out, preferred_element_type=jnp.fl...  28.9 us
    all_to_all x1, waiting for transfers between devices, body(): lax.all_to_all(back, 'exp', split_axis=0, concat_axis=0, tiled=True)  23.3 us
  transfers between devices with their start and end apart: 4, of which 2 were waited for; matrix products, arithmetic and copies ran while one was open for 2% of the time, Pallas kernels for 0%

profile of v1, /device:TPU:1, one launch (start us, length us, event | category | flops | bytes accessed | tf_op | source)
XLA Modules:
  0.0 402.1 jit_solution(15290407687089227919)
XLA Ops:
  6.5 1.1 slice_bitcast_fusion.1
  7.7 4.0 collective-permute-start
  11.7 1.3 collective-permute-start.1
  13.0 1.3 convert_reduce_fusion
  14.2 1.4 fusion.61
  15.6 0.5 broadcast.175
  16.2 1.3 reduce.22
  17.6 0.2 fusion.79
  17.8 1.4 fusion.63
  19.2 1.0 slice_reduce_fusion.8
  20.2 0.1 convert_reduce_fusion.1
  20.4 0.2 fusion.82
  20.6 0.9 fusion.84
  21.6 0.2 maximum_convert_fusion
  21.8 1.7 fusion.119
  23.5 0.3 multiply_reduce_fusion
  23.8 0.2 multiply_convert_fusion
  24.0 1.4 convolution_convert_fusion
  25.4 2.9 reshape.127
  28.3 33.1 %all_to_all.15 = bf16[16,10,2,1280]{3,2,1,0:T(2,128)(2,1)S(1)} all-to-all(bf16[16,10,2,1280]{3,2,1,0:T(2,128)(2,1)} %reshape.127), channel_id=1, replica_groups=mesh['seq'=16,'exp'=16,'dp'=1] {'exp'}, dimensions={0} | all-to-all | bytes 1638400 | tf_op jit(solution)/shard_map/all_to_all | solution.py:93
  61.4 1.0 copy.19
  62.4 7.3 %stack.2 = bf16[16,16,10,2,1280]{4,1,2,3,0:T(8,128)(2,1)} broadcast(bf16[16,10,2,1280]{3,0,1,2:T(8,128)(2,1)} %copy.19), dimensions={1,2,3,4} | broadcast | bytes 13926400 | tf_op jit(solution)/shard_map/stack | solution.py:95
  69.7 156.6 %all_to_all.16 = bf16[16,16,10,2,1280]{4,1,2,3,0:T(8,128)(2,1)S(1)} all-to-all(bf16[16,16,10,2,1280]{4,1,2,3,0:T(8,128)(2,1)} %stack.2), channel_id=1, replica_groups=mesh['seq'=16,'exp'=16,'dp'=1] {'seq'}, dimensions={0} | all-to-all | bytes 26214400 | tf_op jit(solution)/shard_map/all_to_all | solution.py:96
  226.3 5.2 %copy.20 = bf16[16,16,10,2,1280]{4,1,0,2,3:T(8,128)(2,1)} copy(bf16[16,16,10,2,1280]{4,1,2,3,0:T(8,128)(2,1)S(1)} %all_to_all.16) | data formatting | bytes 26214400 | tf_op jit(solution)/shard_map/all_to_all | solution.py:96
  231.5 28.9 %convert_bitcast_fusion = bf16[256,10,2,1280]{3,0,1,2:T(8,128)(2,1)} fusion(bf16[256,10,2,1280]{3,0,1,2:T(8,128)(2,1)} %bitcast.110, f32[2,320]{1,0:T(2,128)S(1)} %copy-done.7, bf16[2,320,1280]{2,1,0:T(8,128)(2,1)S(1)} %copy-done, bf16[2,1280,320]{1,2,0:T(8,128)(2,1)} %param.18), kind=kOutput, calls=%fused_computation | convolution fusion | flops 8503296000 | bytes 29493760 | tf_op jit(solution)/shard_map/kcjf,jfd->kcjd/dot_general | solution.py:104
  260.5 94.8 %reduce-scatter.2.cloned.1.call-done = bf16[16,10,2,1280]{3,0,1,2:T(8,128)(2,1)} async-done(((bf16[256,10,2,1280]{3,0,1,2:T(8,128)(2,1)}), bf16[16,10,2,1280]{3,0,1,2:T(8,128)(2,1)}) %reduce-scatter.2.cloned.1.call-update) | async-done | bytes 819216 | tf_op jit(solution)/shard_map/reduce_scatter | solution.py:103
  355.3 1.3 add_convert_fusion
  356.6 1.7 copy.21
  358.4 7.9 %all-to-all-start.2 = ((bf16[16,10,2,1280]{3,2,1,0:T(2,128)(2,1)}), bf16[16,10,2,1280]{3,2,1,0:T(2,128)(2,1)}, u32[]{:S(2)}, u32[]{:S(2)}) async-start(bf16[16,10,2,1280]{3,2,1,0:T(2,128)(2,1)} %copy.21), calls=%async_computation.3 | async-start | bytes 1638400 | tf_op jit(solution)/shard_map/all_to_all | solution.py:112
  366.3 23.3 %all-to-all-done.2 = bf16[16,10,2,1280]{3,2,1,0:T(2,128)(2,1)} async-done(((bf16[16,10,2,1280]{3,2,1,0:T(2,128)(2,1)}), bf16[16,10,2,1280]{3,2,1,0:T(2,128)(2,1)}, u32[]{:S(2)}, u32[]{:S(2)}) %all-to-all-start.2) | async-done | bytes 819232 | tf_op jit(solution)/shard_map/all_to_all | solution.py:112
  389.7 3.0 reshape.129
  392.7 2.5 fusion.53
  (30 shorter events, 0.3 us)
Async XLA Ops:
  6.5 225.0 %copy-start = (bf16[2,320,1280]{2,1,0:T(8,128)(2,1)S(1)}, bf16[2,320,1280]{2,1,0:T(8,128)(2,1)}, u32[]{:S(2)}) copy-start(bf16[2,320,1280]{2,1,0:T(8,128)(2,1)} %param.20) | copy-start | bytes 4915204
  6.5 15.2 %copy-start.5 = (f32[1280]{0:T(1024)S(1)}, f32[1280]{0:T(1024)}, u32[]{:S(2)}) copy-start(f32[1280]{0:T(1024)} %param.17) | copy-start | bytes 15364
  6.5 348.8 %reduce-scatter.2.cloned.1.call-start = ((), (), s32[]{:S(2)}) async-start(), calls=%async_computation.4 | async-start | bytes 13926400 | tf_op jit(solution)/shard_map/reduce_scatter | solution.py:103
  7.7 12.5 %collective-permute-start = (bf16[1,64,1280]{2,1,0:T(8,128)(2,1)S(1)}, bf16[1,64,1280]{2,1,0:T(8,128)(2,1)S(1)}, u32[]{:S(2)}, u32[]{:S(2)}) collective-permute-start(bf16[1,64,1280]{2,1,0:T(8,128)(2,1)S(1)} %get-tuple-element.16), channel_id=1, source_target_pairs={{0,16},{16,32},{32,48},{48,64},{64,80},{80,96},{96,112},{112,128},... | collective-permute-start | bytes 491528 | tf_op jit(solution)/shard_map/ppermute | solution.py:15
  11.7 8.6 %collective-permute-start.1 = (bf16[1,64,1280]{2,1,0:T(8,128)(2,1)S(1)}, bf16[1,64,1280]{2,1,0:T(8,128)(2,1)S(1)}, u32[]{:S(2)}, u32[]{:S(2)}) collective-permute-start(bf16[1,64,1280]{2,1,0:T(8,128)(2,1)S(1)} %get-tuple-element.17), channel_id=1, source_target_pairs={{16,0},{32,16},{48,32},{64,48},{80,64},{96,80},{112,96},{128,112},... | collective-permute-start | bytes 491528 | tf_op jit(solution)/shard_map/ppermute | solution.py:17
  17.6 4.2 %copy-start.2 = (bf16[1,4,64,1280]{3,2,1,0:T(8,128)(2,1)S(1)}, bf16[1,4,64,1280]{3,2,1,0:T(8,128)(2,1)}, u32[]{:S(2)}) copy-start(bf16[1,4,64,1280]{3,2,1,0:T(8,128)(2,1)} %param.11) | copy-start | bytes 1966084
  21.5 2.2 copy-start.4
  226.3 5.2 %copy-start.7 = (f32[2,320]{1,0:T(2,128)S(1)}, f32[2,320]{1,0:T(2,128)}, u32[]{:S(2)}) copy-start(f32[2,320]{1,0:T(2,128)} %param.19) | copy-start | bytes 7684
  260.5 94.8 %copy-start.3 = (f32[2,1280]{1,0:T(2,128)S(1)}, f32[2,1280]{1,0:T(2,128)}, u32[]{:S(2)}) copy-start(f32[2,1280]{1,0:T(2,128)} %param.21) | copy-start | bytes 30724
  260.5 105.8 %copy-start.6 = (f32[1,4,64]{2,1,0:T(4,128)S(1)}, f32[1,4,64]{2,1,0:T(4,128)}, u32[]{:S(2)}) copy-start(f32[1,4,64]{2,1,0:T(4,128)} %param.13) | copy-start | bytes 3076
  260.5 134.7 %copy-start.1 = (bf16[2,320,1280]{2,1,0:T(8,128)(2,1)S(1)}, bf16[2,320,1280]{2,1,0:T(8,128)(2,1)}, u32[]{:S(2)}) copy-start(bf16[2,320,1280]{2,1,0:T(8,128)(2,1)} %param.20) | copy-start | bytes 4915204
  358.4 31.3 %all-to-all-start.2 = ((bf16[16,10,2,1280]{3,2,1,0:T(2,128)(2,1)}), bf16[16,10,2,1280]{3,2,1,0:T(2,128)(2,1)}, u32[]{:S(2)}, u32[]{:S(2)}) async-start(bf16[16,10,2,1280]{3,2,1,0:T(2,128)(2,1)} %copy.21), calls=%async_computation.3 | async-start | bytes 1638400 | tf_op jit(solution)/shard_map/all_to_all | solution.py:112
Sparse Core Ops, SparseCore 0:
  260.6 94.6 reduce-scatter.1
